TPU v7x, 32 devices: a whole 2x2x4 slice. The times are simulated.
32 devices in a mesh: stream: 4 (over y, x), ctx: 4 (over z), head: 2 (over core).
Axes of the slice: x: 2, y: 2, z: 4, core: 2. Of those that a mesh axis runs over, the one named last changes fastest.
Arguments:
- tokens: bfloat16 [4, 1024, 2048], P('stream', 'ctx'), may hold values from -6 to 6
- doc_lengths: int32 [4, 6], P('stream'), may hold values from 1 to 512, 1024 in all within a row
- ln1_gain: bfloat16 [2048], replicated, may hold values from 0.25 to 1.75
- ln1_bias: bfloat16 [2048], replicated, may hold values from -1.5 to 1.5
- qkv_weight: bfloat16 [3, 2048, 2048], P(None, 'ctx', 'head'), may hold values from -0.125 to 0.125
- qkv_bias: bfloat16 [3, 2048], P(None, 'head'), may hold values from -0.5 to 0.5
- out_weight: bfloat16 [2048, 2048], P('head', 'ctx'), may hold values from -1 to 1
- out_bias: bfloat16 [2048], replicated, may hold values from -3 to 3
- ln2_gain: bfloat16 [2048], replicated, may hold values from 0.25 to 1.75
- ln2_bias: bfloat16 [2048], replicated, may hold values from -1.5 to 1.5
- up_weight: bfloat16 [2048, 8192], P('ctx', 'head'), may hold values from -0.125 to 0.125
- up_bias: bfloat16 [8192], P('head'), may hold values from -1.5 to 1.5
- down_weight: bfloat16 [8192, 2048], P('head', 'ctx'), may hold values from -0.0625 to 0.0625
- down_bias: bfloat16 [2048], replicated, may hold values from -3 to 3
- cotangent: bfloat16 [4, 1024, 2048], P('stream', 'ctx'), may hold values from -6 to 6
Outputs:
- output: bfloat16 [4, 1024, 2048], P('stream', 'ctx')
- input_grad: float32 [4, 1024, 2048], P('stream', 'ctx')
- ln1_gain_grad: float32 [2048], replicated
- ln1_bias_grad: float32 [2048], replicated
- qkv_weight_grad: float32 [3, 2048, 2048], P(None, 'ctx', 'head')
- qkv_bias_grad: float32 [3, 2048], P(None, 'head')
- out_weight_grad: float32 [2048, 2048], P('head', 'ctx')
- out_bias_grad: float32 [2048], replicated
- ln2_gain_grad: float32 [2048], replicated
- ln2_bias_grad: float32 [2048], replicated
- up_weight_grad: float32 [2048, 8192], P('ctx', 'head')
- up_bias_grad: float32 [8192], P('head')
- down_weight_grad: float32 [8192, 2048], P('head', 'ctx')
- down_bias_grad: float32 [2048], replicated
Inputs may be any that keep to these rules, and one draw needn't show every extreme that they name: `doc_lengths`: each sequence's 6 document lengths sum to 1024, the documents lie end to end in the given order, and the longest has exactly 512 tokens.
All inputs are finite; a program needn't handle non-finite values.
Results may differ from a plain program's by a relative error of at most 0.025.
Values may be sent and summed in bfloat16 or wider, within the bound.
A program may use at most 256 MiB of HBM per device.

v0:
```python
from functools import partial
import math
import jax
import jax.numpy as jnp
from jax import lax
from jax.sharding import PartitionSpec as P

HEAD = 256
ROT = 64


def layer_norm(values, gain, offset):
    centre = jnp.mean(values, axis=-1, keepdims=True)
    centred = values - centre
    spread = jnp.mean(centred * centred, axis=-1, keepdims=True)
    return centred * lax.rsqrt(spread + 1e-05) * gain + offset


def rotary(values, angles):
    half = angles.shape[-1]
    cosine = jnp.cos(angles)[:, None, :]
    sine = jnp.sin(angles)[:, None, :]
    first = values[..., :half]
    second = values[..., half : 2 * half]
    return jnp.concatenate(
        [first * cosine - second * sine, second * cosine + first * sine, values[..., 2 * half :]],
        axis=-1,
    )


def doc_starts(doc_sizes, positions):
    ends = jnp.cumsum(doc_sizes)
    starts = ends - doc_sizes
    return jnp.max(jnp.where(starts[None, :] <= positions[:, None], starts[None, :], 0), axis=1)


def per_device(
    tokens,
    doc_lengths,
    ln1_gain,
    ln1_bias,
    qkv_weight,
    qkv_bias,
    out_weight,
    out_bias,
    ln2_gain,
    ln2_bias,
    up_weight,
    up_bias,
    down_weight,
    down_bias,
    cotangent,
):
    inputs = tokens[0].astype(jnp.float32)
    count = inputs.shape[0]
    ctx_count = lax.axis_size("ctx")
    length = count * ctx_count
    positions = lax.axis_index("ctx") * count + jnp.arange(count, dtype=jnp.int32)
    starts = doc_starts(doc_lengths[0], positions)
    frequency = 10000.0 ** (-jnp.arange(0, ROT, 2, dtype=jnp.float32) / ROT)
    angles = (positions - starts).astype(jnp.float32)[:, None] * frequency[None, :]
    scale = HEAD ** (-0.5)
    full_qkv, full_out, full_up, full_down = (
        lax.all_gather(qkv_weight, "ctx", axis=1, tiled=True),
        lax.all_gather(out_weight, "ctx", axis=1, tiled=True),
        lax.all_gather(up_weight, "ctx", axis=0, tiled=True),
        lax.all_gather(down_weight, "ctx", axis=1, tiled=True),
    )
    gain_one = ln1_gain.astype(jnp.float32)
    offset_one = ln1_bias.astype(jnp.float32)
    gain_two = ln2_gain.astype(jnp.float32)
    offset_two = ln2_bias.astype(jnp.float32)
    low_one = layer_norm(inputs, gain_one, offset_one).astype(jnp.bfloat16)
    low_two = layer_norm(inputs, gain_two, offset_two).astype(jnp.bfloat16)
    projected = (
        jnp.einsum("nd,cde->cne", low_one, full_qkv, preferred_element_type=jnp.float32)
        + qkv_bias.astype(jnp.float32)[:, None, :]
    )
    width = projected.shape[2]
    local_heads = width // HEAD
    query = rotary(projected[0].reshape(count, local_heads, HEAD), angles).astype(jnp.bfloat16)
    keys_flat = (
        rotary(projected[1].reshape(count, local_heads, HEAD), angles)
        .reshape(count, width)
        .astype(jnp.bfloat16)
    )
    values_flat = projected[2].astype(jnp.bfloat16)
    all_keys, all_values = (
        lax.all_gather(keys_flat, "ctx", axis=0, tiled=True),
        lax.all_gather(values_flat, "ctx", axis=0, tiled=True),
    )
    block = math.gcd(length, 512)
    block_count = length // block
    key_blocks = all_keys.reshape(block_count, block, local_heads, HEAD)
    value_blocks = all_values.reshape(block_count, block, local_heads, HEAD)
    firsts = jnp.arange(block_count, dtype=jnp.int32) * block

    def block_scores(key_block, first):
        key_index = first + jnp.arange(block, dtype=jnp.int32)
        allowed = (key_index[None, :] <= positions[:, None]) & (
            key_index[None, :] >= starts[:, None]
        )
        scores = (
            jnp.einsum("qhe,khe->hqk", query, key_block, preferred_element_type=jnp.float32) * scale
        )
        return (jnp.where(allowed[None], scores, -1e30), allowed[None])

    def statistics(carry, item):
        running, norm_sum = carry
        key_block, first = item
        masked, allowed = block_scores(key_block, first)
        newest = jnp.maximum(running, jnp.max(masked, axis=-1))
        raised = jnp.where(allowed, jnp.exp(masked - newest[..., None]), 0.0)
        norm_sum = norm_sum * jnp.exp(running - newest) + jnp.sum(raised, axis=-1)
        return ((newest, norm_sum), None)

    initial = (
        jnp.full((local_heads, count), -1e30, jnp.float32),
        jnp.zeros((local_heads, count), jnp.float32),
    )
    (running, norm_sum), _ = lax.scan(statistics, initial, (key_blocks, firsts))
    log_norm = running + jnp.log(norm_sum)

    def share_block(key_block, first):
        masked, allowed = block_scores(key_block, first)
        return jnp.where(allowed, jnp.exp(masked - log_norm[..., None]), 0.0)

    def accumulate(mixed, item):
        key_block, value_block, first = item
        shares_low = share_block(key_block, first).astype(jnp.bfloat16)
        return (
            mixed
            + jnp.einsum(
                "hqk,khe->qhe", shares_low, value_block, preferred_element_type=jnp.float32
            ),
            None,
        )

    mixed, _ = lax.scan(
        accumulate,
        jnp.zeros((count, local_heads, HEAD), jnp.float32),
        (key_blocks, value_blocks, firsts),
    )
    mixed_low = mixed.reshape(count, width).astype(jnp.bfloat16)
    attention = jnp.dot(mixed_low, full_out, preferred_element_type=jnp.float32)
    hidden = jnp.dot(low_two, full_up, preferred_element_type=jnp.float32) + up_bias.astype(
        jnp.float32
    )
    activated = jax.nn.gelu(hidden, approximate=False).astype(jnp.bfloat16)
    branches = attention + jnp.dot(activated, full_down, preferred_element_type=jnp.float32)
    joint = lax.psum(branches.astype(jnp.bfloat16), "head").astype(jnp.float32)
    output = inputs + joint + out_bias.astype(jnp.float32) + down_bias.astype(jnp.float32)
    upstream = cotangent[0]
    down_grad = jnp.dot(activated.T, upstream, preferred_element_type=jnp.float32)
    activated_grad = jnp.dot(upstream, full_down.T, preferred_element_type=jnp.float32)
    _, gelu_back = jax.vjp(partial(jax.nn.gelu, approximate=False), hidden)
    hidden_grad = gelu_back(activated_grad)[0].astype(jnp.bfloat16)
    up_grad = jnp.dot(low_two.T, hidden_grad, preferred_element_type=jnp.float32)
    up_bias_grad = jnp.sum(hidden_grad.astype(jnp.float32), axis=0)
    normed_two_grad = jnp.dot(hidden_grad, full_up.T, preferred_element_type=jnp.float32)
    out_grad = jnp.dot(mixed_low.T, upstream, preferred_element_type=jnp.float32)
    mixed_grad = jnp.dot(upstream, full_out.T, preferred_element_type=jnp.float32).astype(
        jnp.bfloat16
    )
    mixed_grad_heads = mixed_grad.reshape(count, local_heads, HEAD)
    delta = jnp.sum(mixed_grad_heads.astype(jnp.float32) * mixed, axis=-1).T

    def backward_block(query_grad, item):
        key_block, value_block, first = item
        shares = share_block(key_block, first)
        share_grad = jnp.einsum(
            "qhe,khe->hqk", mixed_grad_heads, value_block, preferred_element_type=jnp.float32
        )
        score_grad = (shares * (share_grad - delta[..., None])).astype(jnp.bfloat16)
        query_grad = (
            query_grad
            + jnp.einsum("hqk,khe->qhe", score_grad, key_block, preferred_element_type=jnp.float32)
            * scale
        )
        key_grad = (
            jnp.einsum("hqk,qhe->khe", score_grad, query, preferred_element_type=jnp.float32)
            * scale
        )
        value_grad = jnp.einsum(
            "hqk,qhe->khe",
            shares.astype(jnp.bfloat16),
            mixed_grad_heads,
            preferred_element_type=jnp.float32,
        )
        return (
            query_grad,
            jnp.concatenate(
                [key_grad.reshape(block, width), value_grad.reshape(block, width)], axis=1
            ),
        )

    query_grad, key_terms = lax.scan(
        backward_block,
        jnp.zeros((count, local_heads, HEAD), jnp.float32),
        (key_blocks, value_blocks, firsts),
    )
    own_grads = lax.psum_scatter(
        key_terms.reshape(length, 2 * width).astype(jnp.bfloat16),
        "ctx",
        scatter_dimension=0,
        tiled=True,
    ).astype(jnp.float32)
    query_pre = rotary(query_grad, -angles).reshape(count, width)
    key_pre = rotary(own_grads[:, :width].reshape(count, local_heads, HEAD), -angles).reshape(
        count, width
    )
    projected_grad = jnp.stack([query_pre, key_pre, own_grads[:, width:]]).astype(jnp.bfloat16)
    qkv_grad = jnp.einsum(
        "nd,cne->cde", low_one, projected_grad, preferred_element_type=jnp.float32
    )
    qkv_bias_grad = jnp.sum(projected_grad.astype(jnp.float32), axis=1)
    normed_one_grad = jnp.einsum(
        "cne,cde->nd", projected_grad, full_qkv, preferred_element_type=jnp.float32
    )
    normed_one_grad, normed_two_grad = (
        lax.psum(normed_one_grad.astype(jnp.bfloat16), "head").astype(jnp.float32),
        lax.psum(normed_two_grad.astype(jnp.bfloat16), "head").astype(jnp.float32),
    )
    _, norm_back_one = jax.vjp(layer_norm, inputs, gain_one, offset_one)
    input_one, gain_grad_one, offset_grad_one = norm_back_one(normed_one_grad)
    _, norm_back_two = jax.vjp(layer_norm, inputs, gain_two, offset_two)
    input_two, gain_grad_two, offset_grad_two = norm_back_two(normed_two_grad)
    upstream_wide = upstream.astype(jnp.float32)
    input_grad = upstream_wide + input_one + input_two
    bias_grad = jnp.sum(upstream_wide, axis=0)
    small = lax.psum(
        (
            gain_grad_one,
            offset_grad_one,
            qkv_bias_grad,
            bias_grad,
            gain_grad_two,
            offset_grad_two,
            up_bias_grad,
        ),
        ("stream", "ctx"),
    )
    slices = (
        lax.psum_scatter(
            qkv_grad.astype(jnp.bfloat16), "ctx", scatter_dimension=1, tiled=True
        ).astype(jnp.float32),
        lax.psum_scatter(
            out_grad.astype(jnp.bfloat16), "ctx", scatter_dimension=1, tiled=True
        ).astype(jnp.float32),
        lax.psum_scatter(
            up_grad.astype(jnp.bfloat16), "ctx", scatter_dimension=0, tiled=True
        ).astype(jnp.float32),
        lax.psum_scatter(
            down_grad.astype(jnp.bfloat16), "ctx", scatter_dimension=1, tiled=True
        ).astype(jnp.float32),
    )
    shards = (
        lax.psum(slices[0].astype(jnp.bfloat16), "stream").astype(jnp.float32),
        lax.psum(slices[1].astype(jnp.bfloat16), "stream").astype(jnp.float32),
        lax.psum(slices[2].astype(jnp.bfloat16), "stream").astype(jnp.float32),
        lax.psum(slices[3].astype(jnp.bfloat16), "stream").astype(jnp.float32),
    )
    return (
        output.astype(jnp.bfloat16)[None],
        input_grad[None],
        small[0],
        small[1],
        shards[0],
        small[2],
        shards[1],
        small[3],
        small[4],
        small[5],
        shards[2],
        small[6],
        shards[3],
        small[3],
    )


def solution(mesh):
    in_specs = (
        P("stream", "ctx", None),
        P("stream", None),
        P(),
        P(),
        P(None, "ctx", "head"),
        P(None, "head"),
        P("head", "ctx"),
        P(),
        P(),
        P(),
        P("ctx", "head"),
        P("head"),
        P("head", "ctx"),
        P(),
        P("stream", "ctx", None),
    )
    out_specs = (
        P("stream", "ctx", None),
        P("stream", "ctx", None),
        P(),
        P(),
        P(None, "ctx", "head"),
        P(None, "head"),
        P("head", "ctx"),
        P(),
        P(),
        P(),
        P("ctx", "head"),
        P("head"),
        P("head", "ctx"),
        P(),
    )
    return jax.shard_map(
        per_device, mesh=mesh, in_specs=in_specs, out_specs=out_specs, check_vma=False
    )
```

profile of v0, /device:TPU:0, one launch (start us, length us, event | category | flops | bytes accessed | tf_op | source)
XLA Modules:
  0.0 2362.3 jit_solution(6158996267998633471)
XLA Ops:
  10.8 219.8 %all-gather.8.cloned.1.call-done = bf16[3,2048,1024]{2,1,0:T(8,128)(2,1)} async-done(((bf16[3,512,1024]{2,1,0:T(8,128)(2,1)}), bf16[3,2048,1024]{2,1,0:T(8,128)(2,1)}) %all-gather.8.cloned.1.call-update) | async-done | bytes 12582928 | tf_op jit(solution)/shard_map/all_gather | solution.py:64
  230.6 6.5 add_bitcast_fusion
  244.9 2.1 slice.108
  249.2 61.9 %all-gather.12.cloned.1.call-done = bf16[1024,2048]{1,0:T(8,128)(2,1)} async-done(((bf16[1024,512]{1,0:T(8,128)(2,1)}), bf16[1024,2048]{1,0:T(8,128)(2,1)}) %all-gather.12.cloned.1.call-update) | async-done | bytes 4194320 | tf_op jit(solution)/shard_map/all_gather | solution.py:65
  311.1 3.5 convolution_convert_fusion.4
  315.9 41.9 %all-gather.10.cloned.1.call-done = bf16[1024,1024]{1,0:T(8,128)(2,1)} async-done(((bf16[256,1024]{1,0:T(8,128)(2,1)}), bf16[1024,1024]{1,0:T(8,128)(2,1)}) %all-gather.10.cloned.1.call-update) | async-done | bytes 2097168 | tf_op jit(solution)/shard_map/all_gather | solution.py:89
  357.8 3.3 reshape.405
  362.7 41.8 %all-gather.18.cloned.1.call-done = bf16[1,1024,1024]{2,1,0:T(8,128)(2,1)} async-done(((bf16[1,256,1024]{2,1,0:T(8,128)(2,1)}), bf16[1,1024,1024]{2,1,0:T(8,128)(2,1)}) %all-gather.18.cloned.1.call-update) | async-done | bytes 2097168 | tf_op jit(solution)/shard_map/all_gather | solution.py:90
  404.5 4.5 reshape.404
  409.0 7.8 while.37
  416.8 14.8 while.38
  420.9 3.3 fusion.152
  428.1 3.5 fusion.152
  431.6 2.6 multiply_reduce_fusion
  434.3 29.0 %while.39 = (s32[]{:T(128)}, f32[256,4,256]{0,2,1:T(8,128)}, bf16[2,512,2048]{1,2,0:T(8,128)(2,1)}, bf16[2,512,4,256]{3,1,2,0:T(8,128)(2,1)}, s32[2]{0:T(128)S(1...) while((s32[]{:T(128)}, f32[256,4,256]{0,2,1:T(8,128)}, ...), condition=%wide.region_13.14_spmd.clone, body=%wide.region_12.13_spmd.clone.sunk | while | flops 1352794880 | bytes 31735028 | solution.py:197
  442.3 2.8 fusion.164
  456.7 3.1 fusion.164
  463.3 6.2 copy.113
  471.3 220.1 %all-gather.14.cloned.1.call-done = bf16[2048,4096]{1,0:T(8,128)(2,1)} async-done(((bf16[512,4096]{1,0:T(8,128)(2,1)}), bf16[2048,4096]{1,0:T(8,128)(2,1)}) %all-gather.14.cloned.1.call-update) | async-done | bytes 16777232 | tf_op jit(solution)/shard_map/all_gather | solution.py:66
  691.4 18.6 multiply_convert_fusion
  710.0 267.8 %all-gather.16.cloned.1.call-done = bf16[4096,2048]{1,0:T(8,128)(2,1)} async-done(((bf16[4096,512]{1,0:T(8,128)(2,1)}), bf16[4096,2048]{1,0:T(8,128)(2,1)}) %all-gather.16.cloned.1.call-update) | async-done | bytes 16777232 | tf_op jit(solution)/shard_map/all_gather | solution.py:67
  977.8 8.9 fusion.102
  986.7 2.2 fusion.63
  989.6 19.1 convert_reduce_fusion
  1008.7 12.0 convolution_convert_fusion.3
  1020.7 35.0 %reduce-scatter.6.cloned.1.call-done = bf16[256,2048]{1,0:T(8,128)(2,1)} async-done(((bf16[1024,2048]{1,0:T(8,128)(2,1)}), bf16[256,2048]{1,0:T(8,128)(2,1)}) %reduce-scatter.6.cloned.1.call-update) | async-done | bytes 1048592 | tf_op jit(solution)/shard_map/reduce_scatter | solution.py:202
  1055.7 2.2 fusion.100
  1069.3 2.9 pad_maximum_fusion.4
  1072.2 2.2 stack_reshape.9
  1074.4 9.3 fusion.64
  1083.8 3.3 convolution_convert_fusion.2
  1088.2 8.0 convert_bitcast_fusion
  1096.2 11.0 convolution_convert_fusion.1
  1107.3 9.8 convolution_convert_fusion
  1117.9 2.1 convert_reduce_fusion.1
  1119.9 3.4 fusion.72
  1123.3 4.1 fusion.80
  1127.4 4.3 convert_reduce_fusion.4
  1131.7 56.9 %reduce-scatter.10.cloned.1.call-done = bf16[1024,512]{1,0:T(8,128)(2,1)} async-done(((bf16[1024,2048]{1,0:T(8,128)(2,1)}), bf16[1024,512]{1,0:T(8,128)(2,1)}) %reduce-scatter.10.cloned.1.call-update) | async-done | bytes 1048592 | tf_op jit(solution)/shard_map/reduce_scatter | solution.py:247
  1188.6 214.7 %reduce-scatter.8.cloned.1.call-done = bf16[3,512,1024]{1,2,0:T(8,128)(2,1)} async-done(((bf16[3,2048,1024]{1,2,0:T(8,128)(2,1)}), bf16[3,512,1024]{1,2,0:T(8,128)(2,1)}) %reduce-scatter.8.cloned.1.call-update) | async-done | bytes 3145744 | tf_op jit(solution)/shard_map/reduce_scatter | solution.py:244
  1403.3 283.9 %reduce-scatter.12.cloned.1.call-done = bf16[512,4096]{1,0:T(8,128)(2,1)} async-done(((bf16[2048,4096]{1,0:T(8,128)(2,1)}), bf16[512,4096]{1,0:T(8,128)(2,1)}) %reduce-scatter.12.cloned.1.call-update) | async-done | bytes 4194320 | tf_op jit(solution)/shard_map/reduce_scatter | solution.py:250
  1687.2 283.3 %reduce-scatter.14.cloned.1.call-done = bf16[4096,512]{1,0:T(8,128)(2,1)} async-done(((bf16[4096,2048]{1,0:T(8,128)(2,1)}), bf16[4096,512]{1,0:T(8,128)(2,1)}) %reduce-scatter.14.cloned.1.call-update) | async-done | bytes 4194320 | tf_op jit(solution)/shard_map/reduce_scatter | solution.py:253
  1970.5 116.1 %all-reduce.7.cloned.1.call-done = (f32[2048]{0:T(1024)}, f32[2048]{0:T(1024)}, f32[3,1024]{1,0:T(4,128)}, f32[2048]{0:T(1024)}, f32[2048]{0:T(1024)}, /*index=5*/f32[2048]{0:T(1024)}, f32[4096]{0:T(1024)}) async-done(((f32[2048]{0:T(1024)}, f32[2048]{0:T(1024)}, f32[3,1024]{1,0:T(4,128)}, f32[2048]{0:T(1024)}, f32[2048]{0:T(1024)}, /*index=5*/f32[2048]{0:T(1024)}, f32[4096]{0:T(1024)}), (f32[2048]{0:T(1024)}, ...) | async-done | bytes 69648 | tf_op jit(solution)/shard_map/psum | solution.py:231
  2086.5 245.9 %all-reduce.9.cloned.1.call-done = (bf16[3,512,1024]{1,2,0:T(8,128)(2,1)}, bf16[1024,512]{1,0:T(8,128)(2,1)}, bf16[512,4096]{1,0:T(8,128)(2,1)}, bf16[4096,512]{1,0:T(8,128)(2,1)}) async-done(((bf16[3,512,1024]{1,2,0:T(8,128)(2,1)}, bf16[1024,512]{1,0:T(8,128)(2,1)}, bf16[512,4096]{1,0:T(8,128)(2,1)}, bf16[4096,512]{1,0:T(8,128)(2,1)}), (bf16[3,512,1024]{1,2,0:T(8,128)(2,1)}, bf16[1024,512]{1,0:T(8,128)(2,1)}, ...) | async-done | bytes 12582928 | tf_op jit(solution)/shard_map/psum | solution.py:258
  2332.5 3.0 convert_element_type.189
  2335.5 3.8 copy.118
  2339.2 6.8 convert_element_type.191
  2346.1 4.6 convert_element_type.194
  (239 shorter events, 75.4 us)
Async XLA Ops:
  7.2 1.9 copy-start
  7.2 223.3 %all-gather.8.cloned.1.call-start = ((), (), s32[]{:S(2)}) async-start(), calls=%async_computation.5 | async-start | bytes 15728640 | tf_op jit(solution)/shard_map/all_gather | solution.py:64
  8.0 303.2 %all-gather.12.cloned.1.call-start = ((), (), s32[]{:S(2)}) async-start(), calls=%async_computation.7 | async-start | bytes 5242880 | tf_op jit(solution)/shard_map/all_gather | solution.py:65
  8.7 349.1 %all-gather.10.cloned.1.call-start = ((), (), s32[]{:S(2)}) async-start(), calls=%async_computation.6 | async-start | bytes 2621440 | tf_op jit(solution)/shard_map/all_gather | solution.py:89
  8.8 221.8 %copy-start.14 = (f32[2048]{0:T(1024)}, f32[2048]{0:T(1024)S(1)}, u32[]{:S(2)}) copy-start(f32[2048]{0:T(1024)S(1)} %convert_element_type.155) | copy-start | bytes 24580
  8.8 221.8 %copy-start.30 = (f32[2048]{0:T(1024)}, f32[2048]{0:T(1024)S(1)}, u32[]{:S(2)}) copy-start(f32[2048]{0:T(1024)S(1)} %convert_element_type.156) | copy-start | bytes 24580
  9.4 221.2 %copy-start.16 = (f32[256]{0:T(256)}, f32[256]{0:T(256)S(1)}, u32[]{:S(2)}) copy-start(f32[256]{0:T(256)S(1)} %broadcast_multiply_fusion) | copy-start | bytes 3076
  9.8 220.8 %copy-start.26 = (f32[256]{0:T(256)}, f32[256]{0:T(256)S(1)}, u32[]{:S(2)}) copy-start(f32[256]{0:T(256)S(1)} %fusion.71) | copy-start | bytes 3076
  9.9 220.7 %copy-start.20 = (f32[256]{0:T(256)}, f32[256]{0:T(256)S(1)}, u32[]{:S(2)}) copy-start(f32[256]{0:T(256)S(1)} %fusion.94) | copy-start | bytes 3076
  244.9 159.6 %all-gather.18.cloned.1.call-start = ((), (), s32[]{:S(2)}) async-start(), calls=%async_computation.15 | async-start | bytes 2621440 | tf_op jit(solution)/shard_map/all_gather | solution.py:90
  247.1 64.0 %copy-start.6 = (bf16[1,256,2048]{2,1,0:T(8,128)(2,1)S(1)}, bf16[1,256,2048]{2,1,0:T(8,128)(2,1)}, u32[]{:S(2)}) copy-start(bf16[1,256,2048]{2,1,0:T(8,128)(2,1)} %param.35) | copy-start | bytes 3145732
  247.1 444.3 %all-gather.14.cloned.1.call-start = ((), (), s32[]{:S(2)}) async-start(), calls=%async_computation.8 | async-start | bytes 20971520 | tf_op jit(solution)/shard_map/all_gather | solution.py:66
  247.7 730.1 %all-gather.16.cloned.1.call-start = ((), (), s32[]{:S(2)}) async-start(), calls=%async_computation.9 | async-start | bytes 20971520 | tf_op jit(solution)/shard_map/all_gather | solution.py:67
  248.3 807.4 %reduce-scatter.6.cloned.1.call-start = ((), (), s32[]{:S(2)}) async-start(), calls=%async_computation.10 | async-start | bytes 5242880 | tf_op jit(solution)/shard_map/reduce_scatter | solution.py:202
  434.3 6.5 copy-start.2
  448.7 6.5 copy-start.2
  469.5 221.9 %copy-start.1 = (bf16[1,256,2048]{2,1,0:T(8,128)(2,1)S(1)}, bf16[1,256,2048]{2,1,0:T(8,128)(2,1)}, u32[]{:S(2)}) copy-start(bf16[1,256,2048]{2,1,0:T(8,128)(2,1)} %param.21) | copy-start | bytes 3145732
  469.5 221.9 %copy-start.17 = (f32[256]{0:T(256)S(1)}, f32[256]{0:T(256)}, u32[]{:S(2)}) copy-start(f32[256]{0:T(256)} %copy-done.16) | copy-start | bytes 3076
  469.5 221.9 %copy-start.21 = (f32[256]{0:T(256)S(1)}, f32[256]{0:T(256)}, u32[]{:S(2)}) copy-start(f32[256]{0:T(256)} %copy-done.20) | copy-start | bytes 3076
  469.5 221.9 %copy-start.23 = (f32[4096]{0:T(1024)S(1)}, f32[4096]{0:T(1024)}, u32[]{:S(2)}) copy-start(f32[4096]{0:T(1024)} %convert_element_type.167) | copy-start | bytes 49156
  470.9 649.1 %all-reduce.11.cloned.1.call-start = ((), (), s32[]{:S(2)}) async-start(), calls=%async_computation.18 | async-start | bytes 6291456 | tf_op jit(solution)/shard_map/psum | solution.py:151
  977.8 8.9 copy-start.9
  977.8 8.9 copy-start.42
  986.7 2.3 copy-start.7
  986.7 2.9 copy-start.44
  1083.7 3.5 copy-start.15
  1083.8 3.5 copy-start.18
  1083.8 3.5 copy-start.22
  1083.8 3.4 copy-start.31
  1083.8 104.8 %reduce-scatter.10.cloned.1.call-start = ((), (), s32[]{:S(2)}) async-start(), calls=%async_computation.12 | async-start | bytes 5242880 | tf_op jit(solution)/shard_map/reduce_scatter | solution.py:247
  1087.1 316.2 %reduce-scatter.8.cloned.1.call-start = ((), (), s32[]{:S(2)}) async-start(), calls=%async_computation.11 | async-start | bytes 15728640 | tf_op jit(solution)/shard_map/reduce_scatter | solution.py:244
  1096.2 591.0 %reduce-scatter.12.cloned.1.call-start = ((), (), s32[]{:S(2)}) async-start(), calls=%async_computation.13 | async-start | bytes 20971520 | tf_op jit(solution)/shard_map/reduce_scatter | solution.py:250
  1107.3 863.1 %reduce-scatter.14.cloned.1.call-start = ((), (), s32[]{:S(2)}) async-start(), calls=%async_computation.14 | async-start | bytes 20971520 | tf_op jit(solution)/shard_map/reduce_scatter | solution.py:253
  1117.2 6.1 copy-start.27
  1117.2 969.4 %all-reduce.7.cloned.1.call-start = ((), (), s32[]{:S(2)}) async-start(), calls=%async_computation.16 | async-start | bytes 147456 | tf_op jit(solution)/shard_map/psum | solution.py:231
  1119.9 7.5 copy-start.4
  1119.9 7.5 copy-start.5
  1119.9 7.5 copy-start.13
  1131.7 1200.8 %all-reduce.9.cloned.1.call-start = ((), (), s32[]{:S(2)}) async-start(), calls=%async_computation.17 | async-start | bytes 25165824 | tf_op jit(solution)/shard_map/psum | solution.py:258
  2332.5 3.0 copy-start.10
  2339.2 6.8 copy-start.8
  2346.1 4.7 copy-start.19
  2346.1 5.3 copy-start.35
  2346.1 5.9 copy-start.34
  2346.1 6.5 copy-start.25
  2346.1 7.6 copy-start.33
  2346.1 8.2 copy-start.32
  2346.1 8.8 copy-start.24
  (13 other events, 18.0 us)
Sparse Core Ops, SparseCore 0:
  9.6 220.8 all-gather.7
  232.1 78.9 all-gather.11
  313.3 44.4 all-gather.9
  359.8 44.6 all-gather.17
  405.9 285.4 all-gather.13
  692.8 284.9 all-gather.15
  980.7 74.9 reduce-scatter.5
  1083.9 23.8 all-reduce.10
  1110.6 77.9 reduce-scatter.9
  1190.9 212.3 reduce-scatter.7
  1405.8 281.3 reduce-scatter.11
  1689.4 281.0 reduce-scatter.13
  1979.1 107.3 all-reduce.6
  2090.8 241.6 all-reduce.8
where the time goes:
time: 2370 us; the launch traced here: 2360 us
  waiting for transfers between devices  2090 us (88%)
  matrix products  142 us (6%)
  local copies, waits for them, and re-layouts  63.1 us (3%)
  other arithmetic  49.8 us (2%)
    reduce_scatter x1, waiting for transfers between devices, per_device(): lax.psum_scatter(up_grad.astype(jnp.bfloat16), 'ctx', scatter_dimension=0...  284 us
    reduce_scatter x1, waiting for transfers between devices, per_device(): lax.psum_scatter(down_grad.astype(jnp.bfloat16), 'ctx', scatter_dimension...  283 us
    all_gather x1, waiting for transfers between devices, per_device(): lax.all_gather(down_weight, 'ctx', axis=1, tiled=True)  268 us
    psum x1, waiting for transfers between devices, per_device(): lax.psum(slices[0].astype(jnp.bfloat16), 'stream').astype(jnp.float32)  246 us
    all_gather x1, waiting for transfers between devices, per_device(): lax.all_gather(up_weight, 'ctx', axis=0, tiled=True)  220 us
    all_gather x1, waiting for transfers between devices, per_device(): lax.all_gather(qkv_weight, 'ctx', axis=1, tiled=True)  220 us
    reduce_scatter x1, waiting for transfers between devices, per_device(): lax.psum_scatter(qkv_grad.astype(jnp.bfloat16), 'ctx', scatter_dimension=...  215 us
    psum x1, waiting for transfers between devices, per_device(): lax.psum((gain_grad_one, offset_grad_one, qkv_bias_grad, bias_grad, gain_...  116 us
  transfers between devices with their start and end apart: 14, of which 13 were waited for; matrix products, arithmetic and copies ran while one was open for 8% of the time, Pallas kernels for 0%

commit v1 on v0

--- a/solution.py
+++ b/solution.py
@@ -229,16 +229,19 @@
     input_grad = upstream_wide + input_one + input_two
     bias_grad = jnp.sum(upstream_wide, axis=0)
     small = lax.psum(
-        (
-            gain_grad_one,
-            offset_grad_one,
-            qkv_bias_grad,
-            bias_grad,
-            gain_grad_two,
-            offset_grad_two,
-            up_bias_grad,
+        lax.psum(
+            (
+                gain_grad_one,
+                offset_grad_one,
+                qkv_bias_grad,
+                bias_grad,
+                gain_grad_two,
+                offset_grad_two,
+                up_bias_grad,
+            ),
+            "stream",
         ),
-        ("stream", "ctx"),
+        "ctx",
     )
     slices = (
         lax.psum_scatter(

time: 2370 us -> 2350 us (level)
    psum x1, waiting for transfers between devices: 116 us -> 10.9 us  [per_device(): lax.psum((gain_grad_one, offset_grad_one, qkv_bias_grad, bias_grad, gain_...]
    psum x0 -> x1, waiting for transfers between devices: none -> 38.3 us  [per_device(): lax.psum(lax.psum((gain_grad_one, offset_grad_one, qkv_bias_grad, bias_gr...]
    reduce_scatter x1, waiting for transfers between devices: 56.9 us -> 81.7 us  [per_device(): lax.psum_scatter(out_grad.astype(jnp.bfloat16), 'ctx', scatter_dimension=...]
  transfers between devices with their start and end apart: 14 -> 15, of which waited for: 13 -> 15; matrix products, arithmetic and copies ran while one was open for 8% -> 8% of each run, Pallas kernels for 0% -> 0%
where the time goes in v1:
time: 2350 us; the launch traced here: 2340 us
  waiting for transfers between devices  2070 us (88%)
  matrix products  141 us (6%)
  local copies, waits for them, and re-layouts  62.4 us (3%)
  other arithmetic  49.9 us (2%)
    reduce_scatter x1, waiting for transfers between devices, per_device(): lax.psum_scatter(up_grad.astype(jnp.bfloat16), 'ctx', scatter_dimension=0...  284 us
    reduce_scatter x1, waiting for transfers between devices, per_device(): lax.psum_scatter(down_grad.astype(jnp.bfloat16), 'ctx', scatter_dimension...  284 us
    all_gather x1, waiting for transfers between devices, per_device(): lax.all_gather(down_weight, 'ctx', axis=1, tiled=True)  268 us
    psum x1, waiting for transfers between devices, per_device(): lax.psum(slices[0].astype(jnp.bfloat16), 'stream').astype(jnp.float32)  246 us
    all_gather x1, waiting for transfers between devices, per_device(): lax.all_gather(up_weight, 'ctx', axis=0, tiled=True)  220 us
    all_gather x1, waiting for transfers between devices, per_device(): lax.all_gather(qkv_weight, 'ctx', axis=1, tiled=True)  220 us
    reduce_scatter x1, waiting for transfers between devices, per_device(): lax.psum_scatter(qkv_grad.astype(jnp.bfloat16), 'ctx', scatter_dimension=...  215 us
    reduce_scatter x1, waiting for transfers between devices, per_device(): lax.psum_scatter(out_grad.astype(jnp.bfloat16), 'ctx', scatter_dimension=...  81.7 us
  transfers between devices with their start and end apart: 15, of which 15 were waited for; matrix products, arithmetic and copies ran while one was open for 8% of the time, Pallas kernels for 0%

profile of v1, /device:TPU:0, one launch (start us, length us, event | category | flops | bytes accessed | tf_op | source)
XLA Modules:
  0.0 2340.7 jit_solution(14466024380915834287)
XLA Ops:
  10.8 219.8 %all-gather.8.cloned.1.call-done = bf16[3,2048,1024]{2,1,0:T(8,128)(2,1)} async-done(((bf16[3,512,1024]{2,1,0:T(8,128)(2,1)}), bf16[3,2048,1024]{2,1,0:T(8,128)(2,1)}) %all-gather.8.cloned.1.call-update) | async-done | bytes 12582928 | tf_op jit(solution)/shard_map/all_gather | solution.py:64
  230.6 6.5 add_bitcast_fusion
  249.2 61.9 %all-gather.12.cloned.1.call-done = bf16[1024,2048]{1,0:T(8,128)(2,1)} async-done(((bf16[1024,512]{1,0:T(8,128)(2,1)}), bf16[1024,2048]{1,0:T(8,128)(2,1)}) %all-gather.12.cloned.1.call-update) | async-done | bytes 4194320 | tf_op jit(solution)/shard_map/all_gather | solution.py:65
  311.1 3.5 convolution_convert_fusion.4
  315.9 41.9 %all-gather.10.cloned.1.call-done = bf16[1024,1024]{1,0:T(8,128)(2,1)} async-done(((bf16[256,1024]{1,0:T(8,128)(2,1)}), bf16[1024,1024]{1,0:T(8,128)(2,1)}) %all-gather.10.cloned.1.call-update) | async-done | bytes 2097168 | tf_op jit(solution)/shard_map/all_gather | solution.py:89
  357.8 3.3 reshape.405
  362.7 41.8 %all-gather.18.cloned.1.call-done = bf16[1,1024,1024]{2,1,0:T(8,128)(2,1)} async-done(((bf16[1,256,1024]{2,1,0:T(8,128)(2,1)}), bf16[1,1024,1024]{2,1,0:T(8,128)(2,1)}) %all-gather.18.cloned.1.call-update) | async-done | bytes 2097168 | tf_op jit(solution)/shard_map/all_gather | solution.py:90
  404.5 4.5 reshape.404
  409.0 7.9 while.37
  416.9 14.8 while.38
  420.9 3.3 fusion.152
  428.2 3.5 fusion.152
  431.7 2.7 multiply_reduce_fusion
  434.4 29.1 %while.39 = (s32[]{:T(128)}, f32[256,4,256]{0,2,1:T(8,128)}, bf16[2,512,2048]{1,2,0:T(8,128)(2,1)}, bf16[2,512,4,256]{3,1,2,0:T(8,128)(2,1)}, s32[2]{0:T(128)S(1...) while((s32[]{:T(128)}, f32[256,4,256]{0,2,1:T(8,128)}, ...), condition=%wide.region_13.14_spmd.clone, body=%wide.region_12.13_spmd.clone.sunk | while | flops 1352794880 | bytes 31735028 | solution.py:197
  442.4 2.8 fusion.164
  456.8 3.1 fusion.164
  463.4 6.2 copy.113
  471.2 220.2 %all-gather.14.cloned.1.call-done = bf16[2048,4096]{1,0:T(8,128)(2,1)} async-done(((bf16[512,4096]{1,0:T(8,128)(2,1)}), bf16[2048,4096]{1,0:T(8,128)(2,1)}) %all-gather.14.cloned.1.call-update) | async-done | bytes 16777232 | tf_op jit(solution)/shard_map/all_gather | solution.py:66
  691.4 18.6 multiply_convert_fusion
  710.0 267.8 %all-gather.16.cloned.1.call-done = bf16[4096,2048]{1,0:T(8,128)(2,1)} async-done(((bf16[4096,512]{1,0:T(8,128)(2,1)}), bf16[4096,2048]{1,0:T(8,128)(2,1)}) %all-gather.16.cloned.1.call-update) | async-done | bytes 16777232 | tf_op jit(solution)/shard_map/all_gather | solution.py:67
  977.8 8.9 fusion.102
  986.8 2.2 fusion.63
  989.6 19.4 convert_reduce_fusion
  1009.0 12.0 convolution_convert_fusion.3
  1021.0 34.7 %reduce-scatter.6.cloned.1.call-done = bf16[256,2048]{1,0:T(8,128)(2,1)} async-done(((bf16[1024,2048]{1,0:T(8,128)(2,1)}), bf16[256,2048]{1,0:T(8,128)(2,1)}) %reduce-scatter.6.cloned.1.call-update) | async-done | bytes 1048592 | tf_op jit(solution)/shard_map/reduce_scatter | solution.py:202
  1055.7 2.2 fusion.100
  1069.3 2.9 pad_maximum_fusion.4
  1072.1 2.2 stack_reshape.9
  1074.3 9.3 fusion.64
  1086.1 21.7 all-reduce.15.cloned.1.call-done
  1107.8 3.4 fusion.72
  1111.2 4.1 fusion.80
  1115.3 4.3 convert_reduce_fusion.4
  1119.6 3.3 convolution_convert_fusion.2
  1123.9 7.8 convert_bitcast_fusion
  1131.8 9.9 convolution_convert_fusion.1
  1142.0 9.8 convolution_convert_fusion
  1151.9 10.9 all-reduce.11.cloned.1.call-done
  1162.9 81.7 %reduce-scatter.10.cloned.1.call-done = bf16[1024,512]{1,0:T(8,128)(2,1)} async-done(((bf16[1024,2048]{1,0:T(8,128)(2,1)}), bf16[1024,512]{1,0:T(8,128)(2,1)}) %reduce-scatter.10.cloned.1.call-update) | async-done | bytes 1048592 | tf_op jit(solution)/shard_map/reduce_scatter | solution.py:250
  1244.6 214.8 %reduce-scatter.8.cloned.1.call-done = bf16[3,512,1024]{1,2,0:T(8,128)(2,1)} async-done(((bf16[3,2048,1024]{1,2,0:T(8,128)(2,1)}), bf16[3,512,1024]{1,2,0:T(8,128)(2,1)}) %reduce-scatter.8.cloned.1.call-update) | async-done | bytes 3145744 | tf_op jit(solution)/shard_map/reduce_scatter | solution.py:247
  1459.4 283.6 %reduce-scatter.12.cloned.1.call-done = bf16[512,4096]{1,0:T(8,128)(2,1)} async-done(((bf16[2048,4096]{1,0:T(8,128)(2,1)}), bf16[512,4096]{1,0:T(8,128)(2,1)}) %reduce-scatter.12.cloned.1.call-update) | async-done | bytes 4194320 | tf_op jit(solution)/shard_map/reduce_scatter | solution.py:253
  1743.0 283.6 %reduce-scatter.14.cloned.1.call-done = bf16[4096,512]{1,0:T(8,128)(2,1)} async-done(((bf16[4096,2048]{1,0:T(8,128)(2,1)}), bf16[4096,512]{1,0:T(8,128)(2,1)}) %reduce-scatter.14.cloned.1.call-update) | async-done | bytes 4194320 | tf_op jit(solution)/shard_map/reduce_scatter | solution.py:256
  2026.6 38.3 %all-reduce.9.cloned.1.call-done = (f32[2048]{0:T(1024)}, f32[2048]{0:T(1024)}, f32[3,1024]{1,0:T(4,128)}, f32[2048]{0:T(1024)}, f32[2048]{0:T(1024)}, /*index=5*/f32[2048]{0:T(1024)}, f32[4096]{0:T(1024)}) async-done(((f32[2048]{0:T(1024)}, f32[2048]{0:T(1024)}, f32[3,1024]{1,0:T(4,128)}, f32[2048]{0:T(1024)}, f32[2048]{0:T(1024)}, /*index=5*/f32[2048]{0:T(1024)}, f32[4096]{0:T(1024)}), (f32[2048]{0:T(1024)}, ...) | async-done | bytes 69648 | tf_op jit(solution)/shard_map/psum | solution.py:231
  2064.8 246.0 %all-reduce.13.cloned.1.call-done = (bf16[3,512,1024]{1,2,0:T(8,128)(2,1)}, bf16[1024,512]{1,0:T(8,128)(2,1)}, bf16[512,4096]{1,0:T(8,128)(2,1)}, bf16[4096,512]{1,0:T(8,128)(2,1)}) async-done(((bf16[3,512,1024]{1,2,0:T(8,128)(2,1)}, bf16[1024,512]{1,0:T(8,128)(2,1)}, bf16[512,4096]{1,0:T(8,128)(2,1)}, bf16[4096,512]{1,0:T(8,128)(2,1)}), (bf16[3,512,1024]{1,2,0:T(8,128)(2,1)}, bf16[1024,512]{1,0:T(8,128)(2,1)}, ...) | async-done | bytes 12582928 | tf_op jit(solution)/shard_map/psum | solution.py:261
  2310.9 3.0 convert_element_type.189
  2313.8 3.8 copy.118
  2317.6 6.8 convert_element_type.191
  2324.5 4.6 convert_element_type.194
  (242 shorter events, 79.2 us)
Async XLA Ops:
  7.2 223.3 %all-gather.8.cloned.1.call-start = ((), (), s32[]{:S(2)}) async-start(), calls=%async_computation.5 | async-start | bytes 15728640 | tf_op jit(solution)/shard_map/all_gather | solution.py:64
  8.0 303.2 %all-gather.12.cloned.1.call-start = ((), (), s32[]{:S(2)}) async-start(), calls=%async_computation.7 | async-start | bytes 5242880 | tf_op jit(solution)/shard_map/all_gather | solution.py:65
  8.7 349.1 %all-gather.10.cloned.1.call-start = ((), (), s32[]{:S(2)}) async-start(), calls=%async_computation.6 | async-start | bytes 2621440 | tf_op jit(solution)/shard_map/all_gather | solution.py:89
  8.8 221.8 %copy-start.14 = (f32[2048]{0:T(1024)}, f32[2048]{0:T(1024)S(1)}, u32[]{:S(2)}) copy-start(f32[2048]{0:T(1024)S(1)} %convert_element_type.155) | copy-start | bytes 24580
  8.8 221.8 %copy-start.30 = (f32[2048]{0:T(1024)}, f32[2048]{0:T(1024)S(1)}, u32[]{:S(2)}) copy-start(f32[2048]{0:T(1024)S(1)} %convert_element_type.156) | copy-start | bytes 24580
  9.4 221.2 %copy-start.16 = (f32[256]{0:T(256)}, f32[256]{0:T(256)S(1)}, u32[]{:S(2)}) copy-start(f32[256]{0:T(256)S(1)} %broadcast_multiply_fusion) | copy-start | bytes 3076
  9.8 220.8 %copy-start.26 = (f32[256]{0:T(256)}, f32[256]{0:T(256)S(1)}, u32[]{:S(2)}) copy-start(f32[256]{0:T(256)S(1)} %fusion.71) | copy-start | bytes 3076
  9.9 220.7 %copy-start.20 = (f32[256]{0:T(256)}, f32[256]{0:T(256)S(1)}, u32[]{:S(2)}) copy-start(f32[256]{0:T(256)S(1)} %fusion.94) | copy-start | bytes 3076
  244.9 159.6 %all-gather.18.cloned.1.call-start = ((), (), s32[]{:S(2)}) async-start(), calls=%async_computation.15 | async-start | bytes 2621440 | tf_op jit(solution)/shard_map/all_gather | solution.py:90
  247.1 64.0 %copy-start.6 = (bf16[1,256,2048]{2,1,0:T(8,128)(2,1)S(1)}, bf16[1,256,2048]{2,1,0:T(8,128)(2,1)}, u32[]{:S(2)}) copy-start(bf16[1,256,2048]{2,1,0:T(8,128)(2,1)} %param.35) | copy-start | bytes 3145732
  247.1 444.3 %all-gather.14.cloned.1.call-start = ((), (), s32[]{:S(2)}) async-start(), calls=%async_computation.8 | async-start | bytes 20971520 | tf_op jit(solution)/shard_map/all_gather | solution.py:66
  247.7 730.1 %all-gather.16.cloned.1.call-start = ((), (), s32[]{:S(2)}) async-start(), calls=%async_computation.9 | async-start | bytes 20971520 | tf_op jit(solution)/shard_map/all_gather | solution.py:67
  248.3 807.4 %reduce-scatter.6.cloned.1.call-start = ((), (), s32[]{:S(2)}) async-start(), calls=%async_computation.10 | async-start | bytes 5242880 | tf_op jit(solution)/shard_map/reduce_scatter | solution.py:202
  434.4 6.5 copy-start.2
  448.7 6.5 copy-start.2
  469.6 221.8 %copy-start.1 = (bf16[1,256,2048]{2,1,0:T(8,128)(2,1)S(1)}, bf16[1,256,2048]{2,1,0:T(8,128)(2,1)}, u32[]{:S(2)}) copy-start(bf16[1,256,2048]{2,1,0:T(8,128)(2,1)} %param.21) | copy-start | bytes 3145732
  469.6 221.8 %copy-start.17 = (f32[256]{0:T(256)S(1)}, f32[256]{0:T(256)}, u32[]{:S(2)}) copy-start(f32[256]{0:T(256)} %copy-done.16) | copy-start | bytes 3076
  469.6 221.8 %copy-start.21 = (f32[256]{0:T(256)S(1)}, f32[256]{0:T(256)}, u32[]{:S(2)}) copy-start(f32[256]{0:T(256)} %copy-done.20) | copy-start | bytes 3076
  469.6 221.8 %copy-start.23 = (f32[4096]{0:T(1024)S(1)}, f32[4096]{0:T(1024)}, u32[]{:S(2)}) copy-start(f32[4096]{0:T(1024)} %convert_element_type.167) | copy-start | bytes 49156
  470.9 636.8 %all-reduce.15.cloned.1.call-start = ((), (), s32[]{:S(2)}) async-start(), calls=%async_computation.19 | async-start | bytes 6291456 | tf_op jit(solution)/shard_map/psum | solution.py:151
  977.8 8.9 copy-start.9
  977.8 8.9 copy-start.42
  1074.3 9.6 copy-start.40
  1074.3 9.6 copy-start.41
  1083.7 24.1 %copy-start.15 = (f32[2048]{0:T(1024)S(1)}, f32[2048]{0:T(1024)}, u32[]{:S(2)}) copy-start(f32[2048]{0:T(1024)} %copy-done.14) | copy-start | bytes 24580
  1083.7 24.1 %copy-start.18 = (f32[256]{0:T(256)S(1)}, f32[256]{0:T(256)}, u32[]{:S(2)}) copy-start(f32[256]{0:T(256)} %copy-done.16) | copy-start | bytes 3076
  1083.7 27.5 %copy-start.27 = (f32[256]{0:T(256)S(1)}, f32[256]{0:T(256)}, u32[]{:S(2)}) copy-start(f32[256]{0:T(256)} %copy-done.26) | copy-start | bytes 3076
  1083.7 27.5 %copy-start.22 = (f32[256]{0:T(256)S(1)}, f32[256]{0:T(256)}, u32[]{:S(2)}) copy-start(f32[256]{0:T(256)} %copy-done.20) | copy-start | bytes 3076
  1083.7 79.1 %all-reduce.11.cloned.1.call-start = ((), (), s32[]{:S(2)}) async-start(), calls=%async_computation.17 | async-start | bytes 147456 | tf_op jit(solution)/shard_map/psum | solution.py:232
  1107.8 7.5 copy-start.4
  1107.8 7.5 copy-start.5
  1107.8 7.5 copy-start.13
  1119.6 3.4 copy-start.31
  1119.6 125.0 %reduce-scatter.10.cloned.1.call-start = ((), (), s32[]{:S(2)}) async-start(), calls=%async_computation.12 | async-start | bytes 5242880 | tf_op jit(solution)/shard_map/reduce_scatter | solution.py:250
  1122.9 336.5 %reduce-scatter.8.cloned.1.call-start = ((), (), s32[]{:S(2)}) async-start(), calls=%async_computation.11 | async-start | bytes 15728640 | tf_op jit(solution)/shard_map/reduce_scatter | solution.py:247
  1131.8 611.2 %reduce-scatter.12.cloned.1.call-start = ((), (), s32[]{:S(2)}) async-start(), calls=%async_computation.13 | async-start | bytes 20971520 | tf_op jit(solution)/shard_map/reduce_scatter | solution.py:253
  1141.8 884.8 %reduce-scatter.14.cloned.1.call-start = ((), (), s32[]{:S(2)}) async-start(), calls=%async_computation.14 | async-start | bytes 20971520 | tf_op jit(solution)/shard_map/reduce_scatter | solution.py:256
  1151.9 913.0 %all-reduce.9.cloned.1.call-start = ((), (), s32[]{:S(2)}) async-start(), calls=%async_computation.16 | async-start | bytes 147456 | tf_op jit(solution)/shard_map/psum | solution.py:231
  1162.8 1148.0 %all-reduce.13.cloned.1.call-start = ((), (), s32[]{:S(2)}) async-start(), calls=%async_computation.18 | async-start | bytes 25165824 | tf_op jit(solution)/shard_map/psum | solution.py:261
  2310.9 3.0 copy-start.10
  2317.6 6.8 copy-start.8
  2324.4 4.7 copy-start.19
  2324.4 5.3 copy-start.35
  2324.4 5.9 copy-start.34
  2324.5 6.5 copy-start.25
  2324.5 7.6 copy-start.33
  2324.5 8.2 copy-start.32
  2324.5 8.8 copy-start.24
  (14 other events, 23.7 us)
Sparse Core Ops, SparseCore 0:
  9.6 220.8 all-gather.7
  232.1 78.9 all-gather.11
  313.3 44.4 all-gather.9
  359.8 44.6 all-gather.17
  405.9 285.4 all-gather.13
  692.8 284.9 all-gather.15
  980.7 74.9 reduce-scatter.5
  1083.8 23.8 all-reduce.14
  1119.7 43.0 all-reduce.10
  1165.6 78.9 reduce-scatter.9
  1247.0 212.3 reduce-scatter.7
  1461.6 281.3 reduce-scatter.11
  1745.4 281.0 reduce-scatter.13
  2029.3 35.5 all-reduce.8
  2069.1 241.7 all-reduce.12
